TPU v7x, 256 devices: a whole 4x4x8 slice. The times are simulated.
256 devices in a mesh: dp: 8 (over y, z_lo), fsdp: 32 (over x, z_hi, core).
Axes of the slice: x: 4, y: 4, z: 8 (z_hi: 4, z_lo: 2; z = z_hi * 2 + z_lo), core: 2. Of those that a mesh axis runs over, the one named last changes fastest.
Arguments:
- queries: bfloat16 [49152, 2560], P(('dp', 'fsdp')), may hold values from -8 to 8
- keys: bfloat16 [49152, 2560], P(('dp', 'fsdp')), may hold values from -8 to 8
- values: bfloat16 [49152, 2560], P(('dp', 'fsdp')), may hold values from -6 to 6
- lengths: int32 [32, 8, 4], P('fsdp'), may hold values from 0 to 192, as said below
- normalized_weight: bfloat16 [2560, 5120], P(None, 'fsdp'), may hold values from -1 to 1
- block_scale_codes: int32 [40, 5120], P(None, 'fsdp'), may hold values from 0 to 255
- scale_group_factor: float32 [5, 5120], P(None, 'fsdp'), may hold values from 0.01 to 0.03
- scale_group_offset: float32 [5, 5120], P(None, 'fsdp'), may hold values from 0.005 to 0.015
- adapter_down_weight: bfloat16 [64, 2560], P(None, 'fsdp'), may hold values from -0.125 to 0.125
- adapter_up_weight: bfloat16 [64, 5120], P(None, 'fsdp'), may hold values from -0.75 to 0.75
- cotangent: bfloat16 [49152, 5120], P(('dp', 'fsdp')), may hold values from -24 to 24
Outputs:
- projection_output: bfloat16 [49152, 5120], P(('dp', 'fsdp'))
- attention_gradient: bfloat16 [49152, 2560], P(('dp', 'fsdp'))
- down_grad: float32 [64, 2560], P(None, 'fsdp')
- adapter_up_gradient: float32 [64, 5120], P(None, 'fsdp')
Inputs may be any that keep to these rules, and one draw needn't show every extreme that they name: The 4 lengths of each block sum to 192; zero lengths, if any, come last; some block is a single document of 192 tokens.
All inputs are finite; a program needn't handle non-finite values.
Results may differ from a plain program's by a relative error of at most 0.0059.
Values may be sent and summed in bfloat16 or wider, within the bound.
No kernel may reach another device: no remote copies, remote signals or barrier semaphores. Data moves between devices by JAX's collectives and lax.ppermute only.
A program may use at most 192 MiB of HBM per device.

v0:
```python
import jax
import jax.numpy as jnp
from jax import lax
from jax.sharding import PartitionSpec as P

HEAD_SIZE = 128
QBLOCK = 64
SCALE_GROUP = 8


adapter_scale = 0.25


def joined_along(parts, dim):
    parts = jnp.moveaxis(parts, 0, dim)
    shape = parts.shape
    return parts.reshape(*shape[:dim], shape[dim] * shape[dim + 1], *shape[dim + 2 :])


def gather_together(arrays, axis, dims):
    vector = jnp.concatenate([a.reshape(-1) for a in arrays])
    lines, at, done = (lax.all_gather(vector, axis), 0, [])
    for a, dim in zip(arrays, dims):
        parts = lines[:, at : at + a.size].reshape(-1, *a.shape)
        done.append(joined_along(parts, dim))
        at += a.size
    return tuple(done)


def in_blocks(x, dim, length):
    shape = x.shape
    parts = x.reshape(*shape[:dim], length, shape[dim] // length, *shape[dim + 1 :])
    return jnp.moveaxis(parts, dim, 0)


def sum_at_owner(x, axis, dim):
    length = lax.axis_size(axis)
    parts = lax.all_to_all(in_blocks(x, dim, length), axis, 0, 0, tiled=True)
    return jnp.sum(parts.astype(jnp.float32), axis=0)


def from_everyone(x, axis):
    length = lax.axis_size(axis)
    return lax.all_to_all(jnp.broadcast_to(x[None], (length, *x.shape)), axis, 0, 0, tiled=True)


def over_copies(x, axis):
    everything = from_everyone(x, axis)
    return jnp.sum(everything, axis=0)


def in_one(arrays, axis):
    vector, at, done = (jnp.concatenate([a.reshape(-1) for a in arrays]), 0, [])
    subtotal = over_copies(vector, axis)
    for a in arrays:
        done.append(subtotal[at : at + a.size].reshape(a.shape))
        at += a.size
    return tuple(done)


def dequantize(normalized_weight, block_scale_codes, scale_group_factor, scale_group_offset):
    spread_scale = jnp.repeat(scale_group_factor, SCALE_GROUP, axis=0)
    spread_offset = jnp.repeat(scale_group_offset, SCALE_GROUP, axis=0)
    absmax = spread_scale * (block_scale_codes.astype(jnp.float32) + 1.0) / 256.0 + spread_offset
    return (normalized_weight.astype(jnp.float32) * jnp.repeat(absmax, QBLOCK, axis=0)).astype(
        jnp.bfloat16
    )


def attend(queries, keys, values, doc_lengths):
    tokens = queries.shape[0]
    head_count = queries.shape[1] // HEAD_SIZE
    query_heads = queries.reshape(tokens, head_count, HEAD_SIZE)
    key_heads = keys.reshape(tokens, head_count, HEAD_SIZE)
    value_heads = values.reshape(tokens, head_count, HEAD_SIZE)
    doc_ends = jnp.cumsum(doc_lengths)
    places = jnp.arange(tokens, dtype=jnp.int32)
    segment = jnp.sum((doc_ends[None, :] <= places[:, None]).astype(jnp.int32), axis=1)
    allowed = (segment[:, None] == segment[None, :]) & (places[None, :] <= places[:, None])
    scores = jnp.einsum(
        "qhe,khe->hqk", query_heads, key_heads, preferred_element_type=jnp.float32
    ) * HEAD_SIZE ** (-0.5)
    scores = jnp.where(allowed[None], scores, -jnp.inf)
    row_max = jnp.max(scores, axis=-1, keepdims=True)
    weights = jnp.exp(scores - row_max)
    total = jnp.sum(weights, axis=-1)
    summed = jnp.einsum(
        "hqk,khe->qhe",
        weights.astype(jnp.bfloat16),
        value_heads,
        preferred_element_type=jnp.float32,
    )
    return (
        (summed / jnp.transpose(total)[:, :, None])
        .astype(jnp.bfloat16)
        .reshape(tokens, head_count * HEAD_SIZE)
    )


def apply_columns(attention_output, grad_view, column_piece):
    block_product = jnp.einsum(
        "ti,iabs->tabs", attention_output, column_piece, preferred_element_type=jnp.float32
    )
    backward = jnp.einsum(
        "tabs,iabs->ti", grad_view, column_piece, preferred_element_type=jnp.float32
    )
    return (block_product, backward)


def per_device(
    queries,
    keys,
    values,
    lengths,
    normalized_weight,
    block_scale_codes,
    scale_group_factor,
    scale_group_offset,
    adapter_down_weight,
    adapter_up_weight,
    cotangent,
):
    tokens = queries.shape[0]
    row_index = lax.axis_index("dp")
    own_lengths = lax.dynamic_index_in_dim(lengths[0], row_index, 0, keepdims=False)
    attention_output = attend(queries, keys, values, own_lengths)
    down_full, complete_up_gradient = gather_together(
        (adapter_down_weight, adapter_up_weight), "fsdp", (1, 1)
    )
    fsdp_size = lax.axis_size("fsdp")
    row_size = lax.axis_size("dp")
    local_base = dequantize(
        normalized_weight, block_scale_codes, scale_group_factor, scale_group_offset
    )
    feature_count = local_base.shape[0]
    part_width = local_base.shape[1] // row_size
    base_view = local_base.reshape(feature_count, 1, row_size, part_width)
    grad_view = cotangent.reshape(tokens, fsdp_size, row_size, part_width)
    product, backward = apply_columns(
        attention_output, grad_view, lax.all_gather(base_view, "fsdp", axis=1, tiled=True)
    )
    reduced_activation = jnp.dot(
        attention_output, down_full.T, preferred_element_type=jnp.float32
    ).astype(jnp.bfloat16)
    projection_output = (
        product.reshape(tokens, -1)
        + adapter_scale
        * jnp.dot(reduced_activation, complete_up_gradient, preferred_element_type=jnp.float32)
    ).astype(jnp.bfloat16)
    reduced_gradient = (
        adapter_scale
        * jnp.dot(cotangent, complete_up_gradient.T, preferred_element_type=jnp.float32)
    ).astype(jnp.bfloat16)
    attention_gradient = (
        backward + jnp.dot(reduced_gradient, down_full, preferred_element_type=jnp.float32)
    ).astype(jnp.bfloat16)
    down_part = jnp.dot(reduced_gradient.T, attention_output, preferred_element_type=jnp.float32)
    partial_up_gradient = adapter_scale * jnp.dot(
        reduced_activation.T, cotangent, preferred_element_type=jnp.float32
    )
    down_share, up_share = (
        sum_at_owner(down_part.astype(jnp.bfloat16), "fsdp", 1),
        sum_at_owner(partial_up_gradient.astype(jnp.bfloat16), "fsdp", 1),
    )
    down_grad, adapter_up_gradient = in_one((down_share, up_share), "dp")
    return (projection_output, attention_gradient, down_grad, adapter_up_gradient)


def solution(mesh):
    return jax.shard_map(
        per_device,
        mesh=mesh,
        in_specs=(
            P(("dp", "fsdp"), None),
            P(("dp", "fsdp"), None),
            P(("dp", "fsdp"), None),
            P("fsdp", None, None),
            P(None, "fsdp"),
            P(None, "fsdp"),
            P(None, "fsdp"),
            P(None, "fsdp"),
            P(None, "fsdp"),
            P(None, "fsdp"),
            P(("dp", "fsdp"), None),
        ),
        out_specs=(
            P(("dp", "fsdp"), None),
            P(("dp", "fsdp"), None),
            P(None, "fsdp"),
            P(None, "fsdp"),
        ),
        check_vma=False,
    )
```

profile of v0, /device:TPU:31, one launch (start us, length us, event | category | flops | bytes accessed | tf_op | source)
XLA Modules:
  0.0 325.5 jit_solution(9004267557292624281)
XLA Ops:
  7.2 0.0 copy-start
  7.2 0.0 all-gather.3.cloned.1.call-start
  7.2 0.9 bitcast_add_fusion
  8.1 0.1 copy.77
  8.2 2.2 broadcast_in_dim.40
  10.4 2.9 reshape.172
  13.3 0.0 copy-start.8
  13.3 0.0 copy-start.7
  13.3 0.0 copy-start.6
  13.3 1.3 multiply_convert_fusion
  14.6 0.2 reshape.173
  14.8 1.1 copy.78
  16.0 0.0 all-gather.3.cloned.1.call-update
  16.0 0.2 dynamic-slice_reduce_fusion
  16.2 0.2 reduce-window.8
  16.4 0.1 reshape.174
  16.5 0.1 reshape.175
  16.6 56.2 %all-gather = bf16[491520]{0:T(1024)(128)(2,1)} all-gather(bf16[15360]{0:T(1024)(128)(2,1)S(1)} %pad_maximum_fusion.1), channel_id=2, replica_groups=mesh['dp'=8,'fsdp'=32] {'fsdp'}, dimensions={0}, use_global_device_ids=true | all-gather | bytes 1013760 | tf_op jit(solution)/shard_map/all_gather | solution.py:22
  72.8 2.5 reshape.187
  75.4 2.0 slice.33
  77.3 3.1 reshape.178
  80.4 3.1 copy.81
  83.5 3.3 %reshape.179 = bf16[64,5120]{1,0:T(8,128)(2,1)} reshape(bf16[64,32,160]{2,1,0:T(8,128)(2,1)} %copy.81) | data formatting | bytes 1310720 | tf_op jit(solution)/shard_map/reshape | solution.py:17
  86.9 0.1 convert_reduce_fusion.2
  87.0 0.1 fusion.35
  87.1 1.8 fusion.15
  88.9 0.0 copy-start.9
  88.9 2.1 fusion.4
  91.0 0.9 fusion.5
  91.9 1.8 fusion.27
  93.7 0.9 copy-done.4
  94.7 0.3 convolution_convert_fusion
  95.0 0.6 reshape.181
  95.6 1.0 copy.131
  96.6 9.6 %all-to-all-start = ((bf16[32,64,80]{2,1,0:T(8,128)(2,1)}), bf16[32,64,80]{2,1,0:T(8,128)(2,1)S(1)}, u32[]{:S(2)}, u32[]{:S(2)}) async-start(bf16[32,64,80]{2,1,0:T(8,128)(2,1)} %bitcast.85), calls=%async_computation | async-start | bytes 1048576 | tf_op jit(solution)/shard_map/all_to_all | solution.py:38
  106.2 0.6 reshape.176
  106.8 1.1 copy.80
  108.0 1.8 reshape.177
  109.8 1.6 convolution_convert_fusion.1
  111.4 0.5 fusion.2
  111.9 2.3 reshape.183
  114.2 2.8 copy.130
  117.0 17.7 %all-to-all-done = bf16[32,64,80]{2,1,0:T(8,128)(2,1)S(1)} async-done(((bf16[32,64,80]{2,1,0:T(8,128)(2,1)}), bf16[32,64,80]{2,1,0:T(8,128)(2,1)S(1)}, u32[]{:S(2)}, u32[]{:S(2)}) %all-to-all-start) | async-done | bytes 327712 | tf_op jit(solution)/shard_map/all_to_all | solution.py:38
  134.6 8.3 %all-to-all-start.1 = ((bf16[32,64,160]{2,1,0:T(8,128)(2,1)}), bf16[32,64,160]{2,1,0:T(8,128)(2,1)}, u32[]{:S(2)}, u32[]{:S(2)}) async-start(bf16[32,64,160]{2,1,0:T(8,128)(2,1)} %bitcast.87), calls=%async_computation.1 | async-start | bytes 2097152 | tf_op jit(solution)/shard_map/all_to_all | solution.py:38
  142.9 0.1 convert_reduce_fusion.1
  143.0 0.1 reshape.182
  143.1 54.2 %all-to-all-done.1 = bf16[32,64,160]{2,1,0:T(8,128)(2,1)} async-done(((bf16[32,64,160]{2,1,0:T(8,128)(2,1)}), bf16[32,64,160]{2,1,0:T(8,128)(2,1)}, u32[]{:S(2)}, u32[]{:S(2)}) %all-to-all-start.1) | async-done | bytes 655392 | tf_op jit(solution)/shard_map/all_to_all | solution.py:38
  197.3 1.4 convert_reduce_fusion
  198.8 0.1 reshape.184
  198.9 1.0 broadcast_in_dim.41
  199.9 8.6 %all-to-all-start.2 = ((f32[8,1,15360]{2,1,0:T(1,128)}), f32[8,1,15360]{2,1,0:T(1,128)S(1)}, u32[]{:S(2)}, u32[]{:S(2)}) async-start(f32[8,1,15360]{2,1,0:T(1,128)} %broadcast_in_dim.41), calls=%async_computation.2 | async-start | bytes 983040 | tf_op jit(solution)/shard_map/all_to_all | solution.py:44
  208.5 2.5 copy.82
  211.1 5.5 %reshape.180 = bf16[192,32,8,20]{0,3,2,1:T(8,128)(2,1)} reshape(bf16[192,5120]{0,1:T(8,128)(2,1)} %copy.82) | data formatting | bytes 3932160 | tf_op jit(solution)/shard_map/reshape | solution.py:138
  216.6 10.1 %all-to-all-done.2 = f32[8,1,15360]{2,1,0:T(1,128)S(1)} async-done(((f32[8,1,15360]{2,1,0:T(1,128)}), f32[8,1,15360]{2,1,0:T(1,128)S(1)}, u32[]{:S(2)}, u32[]{:S(2)}) %all-to-all-start.2) | async-done | bytes 491552 | tf_op jit(solution)/shard_map/all_to_all | solution.py:44
  226.7 0.4 reduce_sum.49
  227.0 0.7 reshape.185
  227.7 0.7 reshape.186
  228.4 2.6 all-gather.3.cloned.1.call-done
  231.0 12.1 %convolution_bitcast_fusion = f32[192,2560]{1,0:T(8,128)S(1)} fusion(bf16[2560,32,8,20]{0,2,3,1:T(8,128)(2,1)} %all-gather.3.cloned.1.call-done, bf16[192,32,8,20]{0,3,2,1:T(8,128)(2,1)} %reshape.180), kind=kOutput, calls=%fused_computation.8 | convolution fusion | flops 5033164800 | bytes 30146560 | tf_op jit(solution)/shard_map/tabs,iabs->ti/dot_general | solution.py:104
  243.2 1.4 fusion.3
  244.5 20.0 %copy.79 = bf16[32,8,20,2560]{3,2,1,0:T(8,128)(2,1)} copy(bf16[32,8,20,2560]{3,1,2,0:T(8,128)(2,1)} %bitcast.86) | data formatting | bytes 52428800 | tf_op jit(solution)/shard_map/ti,iabs->tabs/dot_general | solution.py:101
  264.5 34.6 %dot_general.39 = bf16[5120,2560]{1,0:T(8,128)(2,1)} reshape(bf16[32,8,20,2560]{3,2,1,0:T(8,128)(2,1)} %copy.79) | data formatting | bytes 52428800 | tf_op jit(solution)/shard_map/ti,iabs->tabs/dot_general | solution.py:101
  299.1 15.5 %fusion.18 = f32[192,5120]{1,0:T(8,128)} fusion(bf16[5120,2560]{1,0:T(8,128)(2,1)} %dot_general.39, bf16[20,24,8,128]{3,2,1,0:T(8,128)(2,1)S(1)} %copy-done.5), kind=kOutput, calls=%fused_computation.31 | convolution fusion | flops 5033164800 | bytes 31129600 | tf_op jit(solution)/shard_map/ti,iabs->tabs/dot_general | solution.py:101
  314.6 4.1 %fusion.1 = bf16[192,5120]{1,0:T(8,128)(2,1)} fusion(f32[192,5120]{1,0:T(8,128)} %fusion.18, bf16[192,64]{0,1:T(8,128)(2,1)S(1)} %convolution_convert_fusion.1, bf16[64,5120]{1,0:T(8,128)(2,1)S(1)} %copy-done.3), kind=kOutput, calls=%fused_computation.2 | convolution fusion | flops 128778240 | bytes 6578176 | tf_op jit(solution)/shard_map/dot_general | solution.py:148
  (20 shorter events, 0.1 us)
Async XLA Ops:
  7.2 81.7 %copy-start = (bf16[192,2560]{1,0:T(8,128)(2,1)S(1)}, bf16[192,2560]{1,0:T(8,128)(2,1)}, u32[]{:S(2)}) copy-start(bf16[192,2560]{1,0:T(8,128)(2,1)} %param.12) | copy-start | bytes 2949124
  7.2 223.9 %all-gather.3.cloned.1.call-start = ((), (), s32[]{:S(2)}) async-start(), calls=%async_computation.3 | async-start | bytes 27033600 | tf_op jit(solution)/shard_map/all_gather | solution.py:140
  13.3 2.7 copy-start.8
  13.3 3.1 copy-start.7
  13.3 3.1 copy-start.6
  72.8 14.2 %copy-start.2 = (bf16[192,5120]{1,0:T(8,128)(2,1)S(1)}, bf16[192,5120]{1,0:T(8,128)(2,1)}, u32[]{:S(2)}) copy-start(bf16[192,5120]{1,0:T(8,128)(2,1)} %param.21) | copy-start | bytes 5898244
  88.9 3.0 copy-start.9
  93.7 1.0 copy-start.4
  94.6 11.5 %slice-start = ((bf16[32,15360]{1,0:T(8,128)(2,1)}), bf16[32,5120]{1,0:T(8,128)(2,1)S(1)}, s32[]{:S(2)}) async-start(bf16[32,15360]{1,0:T(8,128)(2,1)} %reshape.187), calls=%async_computation.4 | async-start | bytes 655360 | tf_op jit(solution)/shard_map/slice | solution.py:24
  96.6 38.0 %all-to-all-start = ((bf16[32,64,80]{2,1,0:T(8,128)(2,1)}), bf16[32,64,80]{2,1,0:T(8,128)(2,1)S(1)}, u32[]{:S(2)}, u32[]{:S(2)}) async-start(bf16[32,64,80]{2,1,0:T(8,128)(2,1)} %bitcast.85), calls=%async_computation | async-start | bytes 1048576 | tf_op jit(solution)/shard_map/all_to_all | solution.py:38
  134.6 62.7 %all-to-all-start.1 = ((bf16[32,64,160]{2,1,0:T(8,128)(2,1)}), bf16[32,64,160]{2,1,0:T(8,128)(2,1)}, u32[]{:S(2)}, u32[]{:S(2)}) async-start(bf16[32,64,160]{2,1,0:T(8,128)(2,1)} %bitcast.87), calls=%async_computation.1 | async-start | bytes 2097152 | tf_op jit(solution)/shard_map/all_to_all | solution.py:38
  199.9 26.8 %all-to-all-start.2 = ((f32[8,1,15360]{2,1,0:T(1,128)}), f32[8,1,15360]{2,1,0:T(1,128)S(1)}, u32[]{:S(2)}, u32[]{:S(2)}) async-start(f32[8,1,15360]{2,1,0:T(1,128)} %broadcast_in_dim.41), calls=%async_computation.2 | async-start | bytes 983040 | tf_op jit(solution)/shard_map/all_to_all | solution.py:44
  264.5 34.6 %copy-start.5 = (bf16[20,24,8,128]{3,2,1,0:T(8,128)(2,1)S(1)}, bf16[20,24,8,128]{3,2,1,0:T(8,128)(2,1)}, u32[]{:S(2)}) copy-start(bf16[20,24,8,128]{3,2,1,0:T(8,128)(2,1)} %copy-done.4) | copy-start | bytes 2949124
  299.1 15.5 %copy-start.3 = (bf16[64,5120]{1,0:T(8,128)(2,1)S(1)}, bf16[64,5120]{1,0:T(8,128)(2,1)}, u32[]{:S(2)}) copy-start(bf16[64,5120]{1,0:T(8,128)(2,1)} %reshape.179) | copy-start | bytes 1966084
  299.1 19.6 %copy-start.1 = (bf16[192,2560]{1,0:T(8,128)(2,1)S(1)}, bf16[192,2560]{1,0:T(8,128)(2,1)}, u32[]{:S(2)}) copy-start(bf16[192,2560]{1,0:T(8,128)(2,1)} %param.12) | copy-start | bytes 2949124
Sparse Core Ops, SparseCore 0:
  16.1 214.8 all-gather.2
where the time goes:
time: 327 us; the launch traced here: 326 us
  local copies, waits for them, and re-layouts  97.4 us (30%)
  waiting for transfers between devices  84.6 us (26%)
  blocking collectives  56.2 us (17%)
  matrix products  41.1 us (13%)
  starting transfers between devices  26.5 us (8%)
  between operations  14.3 us (4%)
  other arithmetic  5.33 us (2%)
    all_to_all x2, waiting for transfers between devices, sum_at_owner(): parts = lax.all_to_all(in_blocks(x, dim, length), axis, 0, 0, tiled=True)  71.9 us
    all_gather x1, blocking collectives, gather_together(): lines, at, done = (lax.all_gather(vector, axis), 0, [])  56.2 us
    dot_general x2, local copies, waits for them, and re-layouts, apply_columns(): jnp.einsum('ti,iabs->tabs', attention_output, column_piece, preferred_ele...  54.6 us
    all_to_all x2, starting transfers between devices, sum_at_owner(): parts = lax.all_to_all(in_blocks(x, dim, length), axis, 0, 0, tiled=True)  17.8 us
    dot_general x1, matrix products, apply_columns(): jnp.einsum('ti,iabs->tabs', attention_output, column_piece, preferred_ele...  15.5 us
    dot_general x1, matrix products, apply_columns(): jnp.einsum('tabs,iabs->ti', grad_view, column_piece, preferred_element_ty...  12.1 us
    all_to_all x1, waiting for transfers between devices, from_everyone(): lax.all_to_all(jnp.broadcast_to(x[None], (length, *x.shape)), axis, 0, 0,...  10.1 us
    all_to_all x1, starting transfers between devices, from_everyone(): lax.all_to_all(jnp.broadcast_to(x[None], (length, *x.shape)), axis, 0, 0,...  8.63 us
  transfers between devices with their start and end apart: 4, of which 4 were waited for; matrix products, arithmetic and copies ran while one was open for 14% of the time, Pallas kernels for 0%

commit v1 on v0

v1 whole, which is shorter than its diff:
```python
import jax
import jax.numpy as jnp
import numpy as np
from jax import lax
from jax.experimental import pallas as pl
from jax.experimental.pallas import tpu as pltpu
from jax.sharding import Mesh
from jax.sharding import PartitionSpec as P

HEAD = 128
TOK = 192
BLK = 640
COLS = 160
DCOLS = 80
SCALE = 0.25
AX = ("y", "zl", "x", "zh", "c")
DIMS = (4, 2, 4, 4, 2)
REL = (0, -1, 1, 2)
bf16 = jnp.bfloat16
f32 = jnp.float32

T_Y, T_D, T_S, T_F, T_J1, T_I1, T_J2, T_I2, T_J3, T_I3 = 0, 1, 2, 6, 40, 48, 56, 72, 88, 96
T_LEN = 104


def params(mib=48):
    return pltpu.CompilerParams(vmem_limit_bytes=mib << 20)


def coords():
    return [np.unravel_index(d, DIMS) for d in range(256)]


def device_table():
    rows = np.zeros((256, T_LEN), np.int32)
    for n, (y, zl, x, zh, c) in enumerate(coords()):
        r = rows[n]
        r[T_Y], r[T_D] = y, y * 2 + zl
        for k in range(4):
            r[T_S + k] = (zh - k) % 4
        for f in range(32):
            fx, fz, fc = f // 8, (f // 2) % 4, f % 2
            r[T_F + f] = (fc ^ c) * 16 + (fz ^ zh) * 4 + (fx ^ x)

        def tiles(own, v, us):
            kind = c if own else 1 - c
            if kind == 0:
                return [(2 * ((x + u) % 4), (y + v) % 4) for u in us]
            return [(2 * ((x + v) % 4) + 1, (y + u) % 4) for u in us]

        stage1 = tiles(True, 0, REL) + tiles(False, 0, REL)
        stage2 = tiles(True, -1, REL) + tiles(True, 1, REL) + tiles(False, -1, REL) + tiles(False, 1, REL)
        stage3 = tiles(True, 2, REL) + tiles(False, 2, REL)
        for at_j, at_i, stage in ((T_J1, T_I1, stage1), (T_J2, T_I2, stage2), (T_J3, T_I3, stage3)):
            for k, (j, i) in enumerate(stage):
                r[at_j + k], r[at_i + k] = j, i
    return rows


def index_of(y, zl, x, zh, c):
    return int(np.ravel_multi_index((y % 4, zl, x % 4, zh % 4, c), DIMS))


def send(value, target):
    pairs = [(n, index_of(*target(*(int(v) for v in at)))) for n, at in enumerate(coords())]
    return lax.ppermute(value, AX, pairs)


def z_round(value, k):
    return send(value, lambda y, zl, x, zh, c: (y, zl, x, 2 * (zh % 2) + c + k, zh // 2))


def middle(value, k):
    return send(value, lambda y, zl, x, zh, c: (y, zl, x + k, zh, c) if c == 0 else (y + k, zl, x, zh, c))


def outer(value, k):
    return send(value, lambda y, zl, x, zh, c: (y + k, zl, x, zh, c) if c == 0 else (y, zl, x + k, zh, c))


def sibling(value):
    return send(value, lambda y, zl, x, zh, c: (y, zl, x, zh, 1 - c))


def flip(value, axis, bit):
    at = AX.index(axis)

    def target(*place):
        place = list(place)
        place[at] ^= bit
        return place

    return send(value, target)


def nt(a, b):
    return lax.dot_general(a, b, (((1,), (1,)), ((), ())), preferred_element_type=f32)


def nn(a, b):
    return lax.dot_general(a, b, (((1,), (0,)), ((), ())), preferred_element_type=f32)


def tn(a, b):
    return lax.dot_general(a, b, (((0,), (0,)), ((), ())), preferred_element_type=f32)


def eye(n):
    rows = lax.broadcasted_iota(jnp.int32, (n, n), 0)
    cols = lax.broadcasted_iota(jnp.int32, (n, n), 1)
    return jnp.where(rows == cols, 1.0, 0.0).astype(bf16)


def base_body(tab, weight, codes, factor, offset, out):
    y = tab[T_Y]
    parts = []
    for k in range(10):
        b = y * 10 + k
        code = codes[pl.ds(b, 1), :].astype(f32)
        group = b // 8
        absmax = factor[pl.ds(group, 1), :] * (code + 1.0) / 256.0 + offset[pl.ds(group, 1), :]
        parts.append((weight[k * 64 : (k + 1) * 64, :].astype(f32) * absmax).astype(bf16))
    out[...] = nt(eye(COLS), jnp.concatenate(parts, 0)).astype(bf16)


def base_quarter(tab, weight, codes, factor, offset):
    whole = lambda i, tab: (0, 0)
    return pl.pallas_call(
        base_body,
        out_shape=jax.ShapeDtypeStruct((COLS, BLK), bf16),
        grid_spec=pltpu.PrefetchScalarGridSpec(
            num_scalar_prefetch=1,
            grid=(1,),
            in_specs=[
                pl.BlockSpec((BLK, COLS), lambda i, tab: (tab[T_Y], 0)),
                pl.BlockSpec((40, COLS), whole),
                pl.BlockSpec((5, COLS), whole),
                pl.BlockSpec((5, COLS), whole),
            ],
            out_specs=pl.BlockSpec((COLS, BLK), whole),
        ),
        compiler_params=params(),
        name="base_quarter",
    )(tab, weight, codes, factor, offset)


def order_body(tab, a, b, c, d, out, sems):
    copies = [
        pltpu.make_async_copy(src, out.at[pl.ds(tab[T_S + k] * COLS, COLS), :], sems.at[k])
        for k, src in enumerate((a, b, c, d))
    ]
    for copy in copies:
        copy.start()
    for copy in copies:
        copy.wait()


def ordered(tab, blocks):
    anywhere = pl.BlockSpec(memory_space=pl.ANY)
    return pl.pallas_call(
        order_body,
        out_shape=jax.ShapeDtypeStruct((BLK, BLK), bf16),
        grid_spec=pltpu.PrefetchScalarGridSpec(
            num_scalar_prefetch=1,
            grid=(1,),
            in_specs=[anywhere] * 4,
            out_specs=anywhere,
            scratch_shapes=[pltpu.SemaphoreType.DMA((4,))],
        ),
        compiler_params=params(),
        name="ordered",
    )(tab, *blocks)


def attend_body(tab, lens, queries, keys, values, out):
    d = tab[T_D]
    rows = lax.broadcasted_iota(jnp.int32, (TOK, TOK), 0)
    cols = lax.broadcasted_iota(jnp.int32, (TOK, TOK), 1)
    end = jnp.int32(0)
    row_doc = jnp.zeros((TOK, TOK), jnp.int32)
    col_doc = jnp.zeros((TOK, TOK), jnp.int32)
    for k in range(4):
        end = end + lens[d * 4 + k]
        row_doc = row_doc + jnp.where(rows >= end, 1, 0)
        col_doc = col_doc + jnp.where(cols >= end, 1, 0)
    allowed = (row_doc == col_doc) & (cols <= rows)
    for h in range(BLK // HEAD):
        at = slice(h * HEAD, (h + 1) * HEAD)
        scores = nt(queries[:, at], keys[:, at]) * (HEAD ** -0.5)
        scores = jnp.where(allowed, scores, -1e30)
        weights = jnp.exp(scores - jnp.max(scores, axis=-1, keepdims=True))
        total = jnp.sum(weights, axis=-1, keepdims=True)
        out[:, at] = (nn(weights.astype(bf16), values[:, at]) / total).astype(bf16)


def attend(tab, lens, queries, keys, values):
    spec = pl.BlockSpec((TOK, BLK), lambda i, *_: (0, i))
    return pl.pallas_call(
        attend_body,
        out_shape=jax.ShapeDtypeStruct(queries.shape, bf16),
        grid_spec=pltpu.PrefetchScalarGridSpec(
            num_scalar_prefetch=2, grid=(4,), in_specs=[spec] * 3, out_specs=spec
        ),
        compiler_params=params(),
        name="attend",
    )(tab, lens, queries, keys, values)


def low_body(tab, att, cot, gathered, out, grad, keep, give, down_t, up_t):
    unit = eye(256)
    for f in range(32):
        block = gathered[tab[T_F + f]]
        turned = nt(unit, jnp.concatenate([block, block], 0)).astype(bf16)
        down_t[f * DCOLS : (f + 1) * DCOLS, :] = turned[:DCOLS]
        up_t[f * COLS : (f + 1) * COLS, :] = turned[DCOLS : DCOLS + COLS]
    low = jnp.zeros((TOK, 128), f32)
    for i in range(4):
        at = slice(i * BLK, (i + 1) * BLK)
        low = low + nn(att[:, at], down_t[at, :])
    low_grad = jnp.zeros((TOK, 128), f32)
    for j in range(8):
        at = slice(j * BLK, (j + 1) * BLK)
        low_grad = low_grad + nn(cot[:, at], up_t[at, :])
    first = lax.broadcasted_iota(jnp.int32, (TOK, 128), 1) < 64
    low_grad = low_grad * SCALE
    none = jnp.zeros((TOK, 128), f32)
    low_a, low_b = (jnp.where(first, low, none).astype(bf16), jnp.where(first, none, low).astype(bf16))
    lg_a, lg_b = (
        jnp.where(first, low_grad, none).astype(bf16),
        jnp.where(first, none, low_grad).astype(bf16),
    )

    def put(f, lo, hi, value):
        place = tab[T_F + f]

        @pl.when(place < 16)
        def _():
            keep[place, lo:hi, :] = value

        @pl.when(place >= 16)
        def _():
            give[place - 16, lo:hi, :] = value

    half = DCOLS // 2
    for i in range(4):
        at = slice(i * BLK, (i + 1) * BLK)
        grad[i] = nt(lg_a, down_t[at, :])
        a, b = tn(att[:, at], lg_a), tn(att[:, at], lg_b)
        for k in range(8):
            s = k * DCOLS
            put(i * 8 + k, 0, half, a[s : s + half] + b[s + half : s + DCOLS])
    for j in range(8):
        at = slice(j * BLK, (j + 1) * BLK)
        out[j] = nt(low_a, up_t[at, :]) * SCALE
        a, b = tn(cot[:, at], low_a), tn(cot[:, at], low_b)
        for k in range(4):
            s = k * COLS
            put(j * 4 + k, half, half + DCOLS, (a[s : s + DCOLS] + b[s + DCOLS : s + COLS]) * SCALE)


def low_terms(tab, att, cot, gathered):
    return pl.pallas_call(
        low_body,
        out_shape=(
            jax.ShapeDtypeStruct((8, TOK, BLK), f32),
            jax.ShapeDtypeStruct((4, TOK, BLK), f32),
            jax.ShapeDtypeStruct((16, 120, 128), f32),
            jax.ShapeDtypeStruct((16, 120, 128), f32),
        ),
        grid_spec=pltpu.PrefetchScalarGridSpec(
            num_scalar_prefetch=1,
            grid=(1,),
            in_specs=[
                pl.BlockSpec(att.shape, lambda i, tab: (0, 0)),
                pl.BlockSpec(cot.shape, lambda i, tab: (0, 0)),
                pl.BlockSpec(gathered.shape, lambda i, tab: (0, 0, 0)),
            ],
            out_specs=[
                pl.BlockSpec((8, TOK, BLK), lambda i, tab: (0, 0, 0)),
                pl.BlockSpec((4, TOK, BLK), lambda i, tab: (0, 0, 0)),
                pl.BlockSpec((16, 120, 128), lambda i, tab: (0, 0, 0)),
                pl.BlockSpec((16, 120, 128), lambda i, tab: (0, 0, 0)),
            ],
            scratch_shapes=[
                pltpu.VMEM((32 * DCOLS, 128), bf16),
                pltpu.VMEM((32 * COLS, 128), bf16),
            ],
        ),
        compiler_params=params(56),
        name="low_terms",
    )(tab, att, cot, gathered)


def tiles_body(last, starts, at_j, at_i, tab, att, cot, out_in, grad_in, *refs):
    count = len(starts)
    tiles, (out, grad), rest = refs[:count], refs[count : count + 2], refs[count + 2 :]
    if last:
        out_acc, grad_acc, sems = rest
    else:
        out_acc, grad_acc, sems = out, grad, rest[0]
    step = pl.program_id(0)

    @pl.when(step == 0)
    def _():
        first = pltpu.make_async_copy(out_in, out_acc, sems.at[0])
        second = pltpu.make_async_copy(grad_in, grad_acc, sems.at[1])
        first.start()
        second.start()
        first.wait()
        second.wait()

    j, i = tab[at_j + step], tab[at_i + step]
    for k, (start, tile) in enumerate(zip(starts, tiles)):
        @pl.when((step >= start) & (step < start + tile_count(starts, k)))
        def _():
            w = tile[0]
            out_acc[j] = out_acc[j] + nt(att[...], w)
            grad_acc[i] = grad_acc[i] + nn(cot[...], w)

    if last:
        @pl.when(step == pl.num_programs(0) - 1)
        def _():
            for k in range(8):
                out[:, k * BLK : (k + 1) * BLK] = out_acc[k].astype(bf16)
            for k in range(4):
                grad[:, k * BLK : (k + 1) * BLK] = grad_acc[k].astype(bf16)


def tile_count(starts, k):
    return starts.counts[k]


class Starts(tuple):
    counts = ()


def add_tiles(tab, att, cot, sums, arrays, at_j, at_i, last=False):
    counts = [a.shape[0] for a in arrays]
    starts = Starts(int(v) for v in np.cumsum([0] + counts[:-1]))
    starts.counts = tuple(counts)
    anywhere = pl.BlockSpec(memory_space=pl.ANY)

    def tile_spec(start, n):
        return pl.BlockSpec((1, BLK, BLK), lambda s, tab: (jnp.clip(s - start, 0, n - 1), 0, 0))

    acc = [(8, TOK, BLK), (4, TOK, BLK)]
    if last:
        outs = [jax.ShapeDtypeStruct((TOK, 8 * BLK), bf16), jax.ShapeDtypeStruct((TOK, 4 * BLK), bf16)]
        scratch = [pltpu.VMEM(s, f32) for s in acc]
    else:
        outs = [jax.ShapeDtypeStruct(s, f32) for s in acc]
        scratch = []
    return pl.pallas_call(
        lambda *refs: tiles_body(last, starts, at_j, at_i, *refs),
        out_shape=outs,
        grid_spec=pltpu.PrefetchScalarGridSpec(
            num_scalar_prefetch=1,
            grid=(sum(counts),),
            in_specs=[
                pl.BlockSpec((TOK, BLK), lambda s, tab: (0, tab[at_i + s])),
                pl.BlockSpec((TOK, BLK), lambda s, tab: (0, tab[at_j + s])),
                anywhere,
                anywhere,
                *(tile_spec(start, n) for start, n in zip(starts, counts)),
            ],
            out_specs=[pl.BlockSpec(o.shape, lambda s, tab, n=len(o.shape): (0,) * n) for o in outs],
            scratch_shapes=[*scratch, pltpu.SemaphoreType.DMA((2,))],
        ),
        compiler_params=params(56),
        name="tiles",
    )(tab, att, cot, *sums, *arrays)


def per_device(
    table,
    queries,
    keys,
    values,
    lengths,
    weight,
    codes,
    factor,
    offset,
    down,
    up,
    cot,
):
    tab = table.reshape(-1)
    lens = lengths.reshape(-1)

    quarter = base_quarter(tab, weight, codes, factor, offset)
    own_tile = ordered(tab, [z_round(quarter, k) for k in range(4)])

    adapters = jnp.concatenate([down, up, jnp.zeros((64, 16), bf16)], 1)[None]
    for axis, bit in (("x", 1), ("x", 2), ("zh", 1), ("zh", 2), ("c", 1)):
        adapters = jnp.concatenate([adapters, flip(adapters, axis, bit)], 0)

    att = attend(tab, lens, queries, keys, values)

    row = jnp.stack([own_tile, middle(own_tile, 1), middle(own_tile, -1), middle(own_tile, 2)])
    from_less, from_more = outer(row, 1), outer(row, -1)
    far_a, far_b = outer(from_less[:2], 1), outer(from_more[2:], -1)

    out0, grad0, keep, give = low_terms(tab, att, cot, adapters)
    part = keep + flip(give, "c", 1)
    for axis, bit, n in (("zh", 2, 8), ("zh", 1, 4), ("x", 2, 2), ("x", 1, 1)):
        part = part[:n] + flip(part[n:], axis, bit)
    part = part[0]
    for axis, bit in (("y", 1), ("y", 2), ("zl", 1)):
        part = part + flip(part, axis, bit)
    half = DCOLS // 2
    down_grad = jnp.concatenate([part[:half, :64], part[:half, 64:]], 0).T
    up_grad = jnp.concatenate([part[half:, :64], part[half:, 64:]], 0).T

    sums = add_tiles(tab, att, cot, (out0, grad0), [row, sibling(row)], T_J1, T_I1)
    sums = add_tiles(
        tab,
        att,
        cot,
        sums,
        [from_less, from_more, sibling(from_less), sibling(from_more)],
        T_J2,
        T_I2,
    )
    out, grad = add_tiles(
        tab, att, cot, sums, [far_a, far_b, sibling(far_a), sibling(far_b)], T_J3, T_I3, last=True
    )
    return out, grad, down_grad, up_grad


def solution(mesh):
    fine = Mesh(np.asarray(mesh.devices).reshape(DIMS), AX)
    tokens, owners = ("y", "zl", "x", "zh", "c"), ("x", "zh", "c")
    table = device_table()
    mapped = jax.shard_map(
        per_device,
        mesh=fine,
        in_specs=(
            P(tokens, None),
            P(tokens, None),
            P(tokens, None),
            P(tokens, None),
            P(owners, None, None),
            P(None, owners),
            P(None, owners),
            P(None, owners),
            P(None, owners),
            P(None, owners),
            P(None, owners),
            P(tokens, None),
        ),
        out_specs=(
            P(tokens, None),
            P(tokens, None),
            P(None, owners),
            P(None, owners),
        ),
        check_vma=False,
    )
    return lambda *args: mapped(jnp.asarray(table), *args)
```

time: 327 us -> 243 us (0.74)
  local copies, waits for them, and re-layouts: 97.4 us -> 15.8 us
  Pallas kernels: 0 us -> 75.6 us
  blocking collectives: 56.2 us -> 0 us
  matrix products: 41.1 us -> 0 us
  starting transfers between devices: 26.5 us -> 54.3 us
  between operations: 14.3 us -> 1.24 us
  waiting for transfers between devices: 84.6 us -> 89.5 us
    ppermute x0 -> x29, waiting for transfers between devices: none -> 89.5 us  [send(): return lax.ppermute(value, AX, pairs)]
    all_to_all x3 -> x0, waiting for transfers between devices: 82 us -> none  [the longest x2 71.9 us: sum_at_owner(): parts = lax.all_to_all(in_blocks(x, dim, length), axis, 0, 0, tiled=True)]
    pallas_call x0 -> x7, Pallas kernels: none -> 75.6 us  [the longest x3 53.5 us: add_tiles(): pl.pallas_call(lambda *refs: tiles_body(last, starts, at_j, at_i, *refs),...]
    all_gather x1 -> x0, blocking collectives: 56.2 us -> none  [gather_together(): lines, at, done = (lax.all_gather(vector, axis), 0, [])]
    dot_general x2 -> x0, local copies, waits for them, and re-layouts: 54.6 us -> none  [apply_columns(): jnp.einsum('ti,iabs->tabs', attention_output, column_piece, preferred_ele...]
    ppermute x0 -> x29, starting transfers between devices: none -> 54.3 us  [send(): return lax.ppermute(value, AX, pairs)]
    dot_general x10 -> x0, matrix products: 41.1 us -> none  [the longest x1 15.5 us: apply_columns(): jnp.einsum('ti,iabs->tabs', attention_output, column_piece, preferred_ele...]
    all_to_all x3 -> x0, starting transfers between devices: 26.4 us -> none  [the longest x2 17.8 us: sum_at_owner(): parts = lax.all_to_all(in_blocks(x, dim, length), axis, 0, 0, tiled=True)]
  transfers between devices with their start and end apart: 4 -> 29, of which waited for: 4 -> 12; matrix products, arithmetic and copies ran while one was open for 14% -> 6% of each run, Pallas kernels for 0% -> 25%
where the time goes in v1:
time: 243 us; the launch traced here: 241 us
  waiting for transfers between devices  89.5 us (37%)
  Pallas kernels  75.6 us (31%)
  starting transfers between devices  54.3 us (22%)
  local copies, waits for them, and re-layouts  15.8 us (7%)
  other arithmetic  4.94 us (2%)
    ppermute x29, waiting for transfers between devices, send(): return lax.ppermute(value, AX, pairs)  89.5 us
    ppermute x29, starting transfers between devices, send(): return lax.ppermute(value, AX, pairs)  54.3 us
    pallas_call x3, Pallas kernels, add_tiles(): pl.pallas_call(lambda *refs: tiles_body(last, starts, at_j, at_i, *refs),...  53.5 us
    pallas_call x1, Pallas kernels, low_terms(): pl.pallas_call(low_body, out_shape=(jax.ShapeDtypeStruct((8, TOK, BLK), f...  15.3 us
    unnamed x34, local copies, waits for them, and re-layouts  10.8 us
  transfers between devices with their start and end apart: 29, of which 12 were waited for; matrix products, arithmetic and copies ran while one was open for 6% of the time, Pallas kernels for 25%

profile of v1, /device:TPU:31, one launch (start us, length us, event | category | flops | bytes accessed | tf_op | source)
XLA Modules:
  0.0 241.4 jit_solution(16587409685137215157)
XLA Ops:
  0.7 1.5 constant_dynamic-update-slice_fusion.4
  2.2 0.5 collective-permute-start
  2.7 0.7 dynamic-slice_bitcast_fusion.tab.refs_0_
  3.4 1.5 copy.21.weight
  4.9 0.8 copy-done.4
  5.7 0.7 copy-done.6
  6.4 0.7 copy-done.7
  7.1 0.8 base_quarter.1
  7.9 5.7 %collective-permute-start.5 = (bf16[160,640]{1,0:T(8,128)(2,1)S(1)}, bf16[160,640]{1,0:T(8,128)(2,1)S(1)}, u32[]{:S(2)}, u32[]{:S(2)}) collective-permute-start(bf16[160,640]{1,0:T(8,128)(2,1)S(1)} %base_quarter.1), channel_id=1, source_target_pairs={{0,0},{1,2},{2,4},{3,6},{4,1},{5,3},{6,5},{7,7},{8,8},{9,10},{10,1... | collective-permute-start | bytes 614408 | tf_op jit(solution)/shard_map/ppermute | solution.py:66
  13.7 5.8 %collective-permute-start.6 = (bf16[160,640]{1,0:T(8,128)(2,1)S(1)}, bf16[160,640]{1,0:T(8,128)(2,1)S(1)}, u32[]{:S(2)}, u32[]{:S(2)}) collective-permute-start(bf16[160,640]{1,0:T(8,128)(2,1)S(1)} %base_quarter.1), channel_id=1, source_target_pairs={{0,2},{1,4},{2,6},{3,0},{4,3},{5,5},{6,7},{7,1},{8,10},{9,12},{10,... | collective-permute-start | bytes 614408 | tf_op jit(solution)/shard_map/ppermute | solution.py:66
  19.6 7.0 %collective-permute-start.8 = (bf16[160,640]{1,0:T(8,128)(2,1)S(1)}, bf16[160,640]{1,0:T(8,128)(2,1)S(1)}, u32[]{:S(2)}, u32[]{:S(2)}) collective-permute-start(bf16[160,640]{1,0:T(8,128)(2,1)S(1)} %base_quarter.1), channel_id=1, source_target_pairs={{0,6},{1,0},{2,2},{3,4},{4,7},{5,1},{6,3},{7,5},{8,14},{9,8},{10,1... | collective-permute-start | bytes 614408 | tf_op jit(solution)/shard_map/ppermute | solution.py:66
  26.7 0.9 collective-permute-start.1
  27.6 4.4 %collective-permute-done.1 = bf16[2,64,256]{2,1,0:T(8,128)(2,1)S(1)} collective-permute-done((bf16[2,64,256]{2,1,0:T(8,128)(2,1)S(1)}, bf16[2,64,256]{2,1,0:T(8,128)(2,1)S(1)}, u32[]{:S(2)}, u32[]{:S(2)}) %collective-permute-start.1) | collective-permute-done | bytes 65568 | tf_op jit(solution)/shard_map/ppermute | solution.py:66
  32.0 0.1 collective-permute-start.2
  32.2 1.6 ordered.1
  33.9 1.5 collective-permute-start.10
  35.4 1.0 collective-permute-start.11
  36.3 6.4 %collective-permute-done.2 = bf16[4,64,256]{2,1,0:T(8,128)(2,1)S(1)} collective-permute-done((bf16[4,64,256]{2,1,0:T(8,128)(2,1)S(1)}, bf16[4,64,256]{2,1,0:T(8,128)(2,1)S(1)}, u32[]{:S(2)}, u32[]{:S(2)}) %collective-permute-start.2) | collective-permute-done | bytes 131104 | tf_op jit(solution)/shard_map/ppermute | solution.py:66
  42.8 4.3 %collective-permute-start.3 = (bf16[8,64,256]{2,1,0:T(8,128)(2,1)S(1)}, bf16[8,64,256]{2,1,0:T(8,128)(2,1)S(1)}, u32[]{:S(2)}, u32[]{:S(2)}) collective-permute-start(bf16[8,64,256]{2,1,0:T(8,128)(2,1)S(1)} %pad_maximum_fusion.1), channel_id=1, source_target_pairs={{0,4},{1,5},{2,6},{3,7},{4,0},{5,1},{6,2},{7,3},{8,12},{9,13},{10,... | collective-permute-start | bytes 786440 | tf_op jit(solution)/shard_map/ppermute | solution.py:66
  47.1 0.6 constant_dynamic-update-slice_fusion.3
  47.7 0.6 constant_dynamic-update-slice_fusion.2
  48.3 0.7 constant_dynamic-update-slice_fusion.1
  49.0 6.9 %collective-permute-done.3 = bf16[8,64,256]{2,1,0:T(8,128)(2,1)S(1)} collective-permute-done((bf16[8,64,256]{2,1,0:T(8,128)(2,1)S(1)}, bf16[8,64,256]{2,1,0:T(8,128)(2,1)S(1)}, u32[]{:S(2)}, u32[]{:S(2)}) %collective-permute-start.3) | collective-permute-done | bytes 262176 | tf_op jit(solution)/shard_map/ppermute | solution.py:66
  55.9 0.7 constant_dynamic-update-slice_fusion
  56.6 4.2 %collective-permute-start.4 = (bf16[16,64,256]{2,1,0:T(8,128)(2,1)}, bf16[16,64,256]{2,1,0:T(8,128)(2,1)S(1)}, u32[]{:S(2)}, u32[]{:S(2)}) collective-permute-start(bf16[16,64,256]{2,1,0:T(8,128)(2,1)} %get-tuple-element.34), channel_id=1, source_target_pairs={{0,1},{1,0},{2,3},{3,2},{4,5},{5,4},{6,7},{7,6},{8,9},{9,8},{10,11... | collective-permute-start | bytes 1572872 | tf_op jit(solution)/shard_map/ppermute | solution.py:66
  60.9 2.0 pad_maximum_fusion.refs_5_
  62.9 0.2 collective-permute-start.13
  63.1 1.3 collective-permute-start.14
  64.5 4.3 %attend.1.att.refs_1_ = bf16[192,2560]{1,0:T(8,128)(2,1)S(1)} custom-call(s32[104]{0:T(128)S(1)} %dynamic-slice_bitcast_fusion.tab.refs_0_, s32[32]{0:T(128)S(1)} %reshape.16.lens, bf16[192,2560]{1,0:T(8,128)(2,1)S(1)} %copy-done.1, bf16[192,2560]{1,0:T(8,128)(2,1)S(1)} %copy-done.2, bf16[192,2560]{1,0:T(8,128)(2,1)S(1)} %copy-done.3), custom_call_target="tpu_custom_call" | custom-call | tf_op jit(solution)/shard_map/attend/pallas_call | solution.py:198
  68.8 0.9 copy-done
  69.8 1.0 copy-done.11
  70.9 15.3 %low_terms.1 = (f32[8,192,640]{2,1,0:T(8,128)}, f32[4,192,640]{2,1,0:T(8,128)}, f32[16,120,128]{2,1,0:T(8,128)}, f32[16,120,128]{2,1,0:T(8,128)}) custom-call(s32[104]{0:T(128)} %copy-done.5, bf16[192,2560]{1,0:T(8,128)(2,1)} %copy-done, bf16[192,5120]{1,0:T(8,128)(2,1)} %refs_2_.5, bf16[32,64,256]{2,1,0:T(8,128)(2,1)} %copy-done.11), custom_call_target="tpu_custom_call" | custom-call | tf_op jit(solution)/shard_map/low_terms/pallas_call | solution.py:262
  86.2 7.3 %collective-permute-start.21 = (f32[16,120,128]{2,1,0:T(8,128)}, f32[16,120,128]{2,1,0:T(8,128)S(1)}, u32[]{:S(2)}, u32[]{:S(2)}) collective-permute-start(f32[16,120,128]{2,1,0:T(8,128)} %get-tuple-element.23), channel_id=1, source_target_pairs={{0,1},{1,0},{2,3},{3,2},{4,5},{5,4},{6,7},{7,6},{8,9},{9,8},{10,11... | collective-permute-start | bytes 2949128 | tf_op jit(solution)/shard_map/ppermute | solution.py:66
  93.5 2.4 collective-permute-done.21
  95.9 1.3 add.24
  97.3 0.3 collective-permute-start.22
  97.5 26.8 %collective-permute-done.22 = f32[8,120,128]{2,1,0:T(8,128)S(1)} collective-permute-done((f32[8,120,128]{2,1,0:T(8,128)S(1)}, f32[8,120,128]{2,1,0:T(8,128)S(1)}, u32[]{:S(2)}, u32[]{:S(2)}) %collective-permute-start.22) | collective-permute-done | bytes 491552 | tf_op jit(solution)/shard_map/ppermute | solution.py:66
  124.4 0.1 collective-permute-start.23
  124.5 9.6 %collective-permute-done.23 = f32[4,120,128]{2,1,0:T(8,128)S(1)} collective-permute-done((f32[4,120,128]{2,1,0:T(8,128)S(1)}, f32[4,120,128]{2,1,0:T(8,128)S(1)}, u32[]{:S(2)}, u32[]{:S(2)}) %collective-permute-start.23) | collective-permute-done | bytes 245792 | tf_op jit(solution)/shard_map/ppermute | solution.py:66
  134.1 0.9 collective-permute-start.24
  135.0 4.4 %collective-permute-done.24 = f32[2,120,128]{2,1,0:T(8,128)S(1)} collective-permute-done((f32[2,120,128]{2,1,0:T(8,128)S(1)}, f32[2,120,128]{2,1,0:T(8,128)S(1)}, u32[]{:S(2)}, u32[]{:S(2)}) %collective-permute-start.24) | collective-permute-done | bytes 122912 | tf_op jit(solution)/shard_map/ppermute | solution.py:66
  139.5 0.1 collective-permute-start.25
  139.6 3.1 %collective-permute-done.25 = f32[1,120,128]{2,1,0:T(8,128)S(1)} collective-permute-done((f32[1,120,128]{2,1,0:T(8,128)S(1)}, f32[1,120,128]{2,1,0:T(8,128)S(1)}, u32[]{:S(2)}, u32[]{:S(2)}) %collective-permute-start.25) | collective-permute-done | bytes 61472 | tf_op jit(solution)/shard_map/ppermute | solution.py:66
  142.6 0.2 collective-permute-start.26
  142.8 3.0 %collective-permute-done.26 = f32[120,128]{1,0:T(8,128)S(1)} collective-permute-done((f32[120,128]{1,0:T(8,128)S(1)}, f32[120,128]{1,0:T(8,128)S(1)}, u32[]{:S(2)}, u32[]{:S(2)}) %collective-permute-start.26) | collective-permute-done | bytes 61472 | tf_op jit(solution)/shard_map/ppermute | solution.py:66
  145.8 1.3 collective-permute-start.27
  147.1 3.7 %collective-permute-done.27 = f32[120,128]{1,0:T(8,128)S(1)} collective-permute-done((f32[120,128]{1,0:T(8,128)S(1)}, f32[120,128]{1,0:T(8,128)S(1)}, u32[]{:S(2)}, u32[]{:S(2)}) %collective-permute-start.27) | collective-permute-done | bytes 61472 | tf_op jit(solution)/shard_map/ppermute | solution.py:66
  150.8 0.1 collective-permute-start.28
  150.9 5.8 %collective-permute-start.12 = (bf16[4,640,640]{2,1,0:T(8,128)(2,1)}, bf16[4,640,640]{2,1,0:T(8,128)(2,1)}, u32[]{:S(2)}, u32[]{:S(2)}) collective-permute-start(bf16[4,640,640]{2,1,0:T(8,128)(2,1)} %pad_maximum_fusion.refs_5_), channel_id=1, source_target_pairs={{0,1},{1,0},{2,3},{3,2},{4,5},{5,4},{6,7},{7,6},{8,9},{9,8},{10,11... | collective-permute-start | bytes 9830408 | tf_op jit(solution)/shard_map/ppermute | solution.py:66
  156.7 0.1 collective-permute-start.15
  156.8 1.6 slice.56
  158.4 0.5 collective-permute-start.16
  158.9 1.6 slice.57
  160.5 1.5 collective-permute-start.18
  162.0 17.2 %collective-permute-done.17.refs_5_ = bf16[2,640,640]{2,1,0:T(8,128)(2,1)} collective-permute-done((bf16[2,640,640]{2,1,0:T(8,128)(2,1)S(1)}, bf16[2,640,640]{2,1,0:T(8,128)(2,1)}, u32[]{:S(2)}, u32[]{:S(2)}) %collective-permute-start.17) | collective-permute-done | bytes 1638432 | tf_op jit(solution)/shard_map/ppermute | solution.py:66
  179.3 1.2 collective-permute-start.19
  180.4 1.7 collective-permute-done.18.refs_6_
  182.2 2.2 collective-permute-start.20
  184.5 0.7 copy.23
  185.3 0.7 copy.22
  186.0 15.1 %tiles.3 = (f32[8,192,640]{2,1,0:T(8,128)}, f32[4,192,640]{2,1,0:T(8,128)}) custom-call(s32[104]{0:T(128)} %copy-done.5, bf16[192,2560]{1,0:T(8,128)(2,1)} %copy-done, bf16[192,5120]{1,0:T(8,128)(2,1)} %refs_2_.5, f32[8,192,640]{2,1,0:T(8,128)} %get-tuple-element.14.refs_3_, f32[4,192,640]{2,1,0:T(8,128)} %get-tuple-element.15.refs_4_, ...), custom_call_target="tpu_custom_call" | custom-call | tf_op jit(solution)/shard_map/tiles/pallas_call | solution.py:353
  201.2 1.7 copy-done.8
  202.8 23.5 %tiles.4 = (f32[8,192,640]{2,1,0:T(8,128)}, f32[4,192,640]{2,1,0:T(8,128)}) custom-call(s32[104]{0:T(128)} %copy-done.5, bf16[192,2560]{1,0:T(8,128)(2,1)} %copy-done, bf16[192,5120]{1,0:T(8,128)(2,1)} %refs_2_.5, f32[8,192,640]{2,1,0:T(8,128)} %get-tuple-element.16.refs_3_, f32[4,192,640]{2,1,0:T(8,128)} %get-tuple-element.17.refs_4_, ...), custom_call_target="tpu_custom_call" | custom-call | tf_op jit(solution)/shard_map/tiles/pallas_call | solution.py:353
  226.3 14.9 %tiles.5 = (bf16[192,5120]{1,0:T(8,128)(2,1)}, bf16[192,2560]{1,0:T(8,128)(2,1)}) custom-call(s32[104]{0:T(128)} %copy-done.5, bf16[192,2560]{1,0:T(8,128)(2,1)} %copy-done, bf16[192,5120]{1,0:T(8,128)(2,1)} %refs_2_.5, f32[8,192,640]{2,1,0:T(8,128)} %get-tuple-element.18.refs_3_, f32[4,192,640]{2,1,0:T(8,128)} %get-tuple-element.19.refs_4_, ...), custom_call_target="tpu_custom_call" | custom-call | tf_op jit(solution)/shard_map/tiles/pallas_call | solution.py:353
  (64 shorter events, 1.0 us)
Async XLA Ops:
  2.2 24.5 %collective-permute-start = (bf16[1,64,256]{2,1,0:T(8,128)(2,1)S(1)}, bf16[1,64,256]{2,1,0:T(8,128)(2,1)S(1)}, u32[]{:S(2)}, u32[]{:S(2)}) collective-permute-start(bf16[1,64,256]{2,1,0:T(8,128)(2,1)S(1)} %get-tuple-element.33), channel_id=1, source_target_pairs={{0,8},{1,9},{2,10},{3,11},{4,12},{5,13},{6,14},{7,15},{8,0},{9,1},... | collective-permute-start | bytes 98312 | tf_op jit(solution)/shard_map/ppermute | solution.py:66
  3.4 61.1 %copy-start.5 = (s32[104]{0:T(128)}, s32[104]{0:T(128)S(1)}, u32[]{:S(2)}) copy-start(s32[104]{0:T(128)S(1)} %dynamic-slice_bitcast_fusion.tab.refs_0_) | copy-start | bytes 1252
  4.9 0.8 copy-start.4
  5.7 0.7 copy-start.6
  6.4 0.7 copy-start.7
  7.9 24.2 %collective-permute-start.5 = (bf16[160,640]{1,0:T(8,128)(2,1)S(1)}, bf16[160,640]{1,0:T(8,128)(2,1)S(1)}, u32[]{:S(2)}, u32[]{:S(2)}) collective-permute-start(bf16[160,640]{1,0:T(8,128)(2,1)S(1)} %base_quarter.1), channel_id=1, source_target_pairs={{0,0},{1,2},{2,4},{3,6},{4,1},{5,3},{6,5},{7,7},{8,8},{9,10},{10,1... | collective-permute-start | bytes 614408 | tf_op jit(solution)/shard_map/ppermute | solution.py:66
  13.7 18.5 %collective-permute-start.6 = (bf16[160,640]{1,0:T(8,128)(2,1)S(1)}, bf16[160,640]{1,0:T(8,128)(2,1)S(1)}, u32[]{:S(2)}, u32[]{:S(2)}) collective-permute-start(bf16[160,640]{1,0:T(8,128)(2,1)S(1)} %base_quarter.1), channel_id=1, source_target_pairs={{0,2},{1,4},{2,6},{3,0},{4,3},{5,5},{6,7},{7,1},{8,10},{9,12},{10,... | collective-permute-start | bytes 614408 | tf_op jit(solution)/shard_map/ppermute | solution.py:66
  19.5 12.6 %collective-permute-start.7 = (bf16[160,640]{1,0:T(8,128)(2,1)S(1)}, bf16[160,640]{1,0:T(8,128)(2,1)S(1)}, u32[]{:S(2)}, u32[]{:S(2)}) collective-permute-start(bf16[160,640]{1,0:T(8,128)(2,1)S(1)} %base_quarter.1), channel_id=1, source_target_pairs={{0,4},{1,6},{2,0},{3,2},{4,5},{5,7},{6,1},{7,3},{8,12},{9,14},{10,... | collective-permute-start | bytes 614408 | tf_op jit(solution)/shard_map/ppermute | solution.py:66
  19.6 12.5 %collective-permute-start.8 = (bf16[160,640]{1,0:T(8,128)(2,1)S(1)}, bf16[160,640]{1,0:T(8,128)(2,1)S(1)}, u32[]{:S(2)}, u32[]{:S(2)}) collective-permute-start(bf16[160,640]{1,0:T(8,128)(2,1)S(1)} %base_quarter.1), channel_id=1, source_target_pairs={{0,6},{1,0},{2,2},{3,4},{4,7},{5,1},{6,3},{7,5},{8,14},{9,8},{10,1... | collective-permute-start | bytes 614408 | tf_op jit(solution)/shard_map/ppermute | solution.py:66
  26.7 5.3 %collective-permute-start.1 = (bf16[2,64,256]{2,1,0:T(8,128)(2,1)S(1)}, bf16[2,64,256]{2,1,0:T(8,128)(2,1)S(1)}, u32[]{:S(2)}, u32[]{:S(2)}) collective-permute-start(bf16[2,64,256]{2,1,0:T(8,128)(2,1)S(1)} %pad_maximum_fusion.3), channel_id=1, source_target_pairs={{0,16},{1,17},{2,18},{3,19},{4,20},{5,21},{6,22},{7,23},{8,24},{9,... | collective-permute-start | bytes 196616 | tf_op jit(solution)/shard_map/ppermute | solution.py:66
  32.0 10.7 %collective-permute-start.2 = (bf16[4,64,256]{2,1,0:T(8,128)(2,1)S(1)}, bf16[4,64,256]{2,1,0:T(8,128)(2,1)S(1)}, u32[]{:S(2)}, u32[]{:S(2)}) collective-permute-start(bf16[4,64,256]{2,1,0:T(8,128)(2,1)S(1)} %pad_maximum_fusion.2), channel_id=1, source_target_pairs={{0,2},{1,3},{2,0},{3,1},{4,6},{5,7},{6,4},{7,5},{8,10},{9,11},{10,... | collective-permute-start | bytes 393224 | tf_op jit(solution)/shard_map/ppermute | solution.py:66
  33.8 27.0 %collective-permute-start.9 = (bf16[640,640]{1,0:T(8,128)(2,1)S(1)}, bf16[640,640]{1,0:T(8,128)(2,1)S(1)}, u32[]{:S(2)}, u32[]{:S(2)}) collective-permute-start(bf16[640,640]{1,0:T(8,128)(2,1)S(1)} %ordered.1), channel_id=1, source_target_pairs={{0,8},{1,65},{2,10},{3,67},{4,12},{5,69},{6,14},{7,71},{8,16},{9,7... | collective-permute-start | bytes 2457608 | tf_op jit(solution)/shard_map/ppermute | solution.py:66
  33.9 26.9 %collective-permute-start.10 = (bf16[640,640]{1,0:T(8,128)(2,1)S(1)}, bf16[640,640]{1,0:T(8,128)(2,1)S(1)}, u32[]{:S(2)}, u32[]{:S(2)}) collective-permute-start(bf16[640,640]{1,0:T(8,128)(2,1)S(1)} %ordered.1), channel_id=1, source_target_pairs={{0,24},{1,193},{2,26},{3,195},{4,28},{5,197},{6,30},{7,199},{8,0},... | collective-permute-start | bytes 2457608 | tf_op jit(solution)/shard_map/ppermute | solution.py:66
  35.4 25.5 %collective-permute-start.11 = (bf16[640,640]{1,0:T(8,128)(2,1)S(1)}, bf16[640,640]{1,0:T(8,128)(2,1)S(1)}, u32[]{:S(2)}, u32[]{:S(2)}) collective-permute-start(bf16[640,640]{1,0:T(8,128)(2,1)S(1)} %ordered.1), channel_id=1, source_target_pairs={{0,16},{1,129},{2,18},{3,131},{4,20},{5,133},{6,22},{7,135},{8,24}... | collective-permute-start | bytes 2457608 | tf_op jit(solution)/shard_map/ppermute | solution.py:66
  42.8 13.1 %collective-permute-start.3 = (bf16[8,64,256]{2,1,0:T(8,128)(2,1)S(1)}, bf16[8,64,256]{2,1,0:T(8,128)(2,1)S(1)}, u32[]{:S(2)}, u32[]{:S(2)}) collective-permute-start(bf16[8,64,256]{2,1,0:T(8,128)(2,1)S(1)} %pad_maximum_fusion.1), channel_id=1, source_target_pairs={{0,4},{1,5},{2,6},{3,7},{4,0},{5,1},{6,2},{7,3},{8,12},{9,13},{10,... | collective-permute-start | bytes 786440 | tf_op jit(solution)/shard_map/ppermute | solution.py:66
  56.6 6.3 %copy-start.9 = (bf16[32,64,256]{2,1,0:T(8,128)(2,1)}, bf16[32,64,256]{2,1,0:T(8,128)(2,1)S(1)}, u32[]{:S(2)}) copy-start(bf16[32,64,256]{2,1,0:T(8,128)(2,1)S(1)} %get-tuple-element.35) | copy-start | bytes 3145732
  56.6 13.2 %collective-permute-start.4 = (bf16[16,64,256]{2,1,0:T(8,128)(2,1)}, bf16[16,64,256]{2,1,0:T(8,128)(2,1)S(1)}, u32[]{:S(2)}, u32[]{:S(2)}) collective-permute-start(bf16[16,64,256]{2,1,0:T(8,128)(2,1)} %get-tuple-element.34), channel_id=1, source_target_pairs={{0,1},{1,0},{2,3},{3,2},{4,5},{5,4},{6,7},{7,6},{8,9},{9,8},{10,11... | collective-permute-start | bytes 1572872 | tf_op jit(solution)/shard_map/ppermute | solution.py:66
  60.9 3.5 %copy-start.12 = (s32[1,8,4]{1,2,0:T(4,128)S(1)}, s32[1,8,4]{1,2,0:T(4,128)}, u32[]{:S(2)}) copy-start(s32[1,8,4]{1,2,0:T(4,128)} %param.15) | copy-start | bytes 388
  60.9 3.6 %copy-start.1 = (bf16[192,2560]{1,0:T(8,128)(2,1)S(1)}, bf16[192,2560]{1,0:T(8,128)(2,1)}, u32[]{:S(2)}) copy-start(bf16[192,2560]{1,0:T(8,128)(2,1)} %queries.1) | copy-start | bytes 2949124
  60.9 3.6 %copy-start.2 = (bf16[192,2560]{1,0:T(8,128)(2,1)S(1)}, bf16[192,2560]{1,0:T(8,128)(2,1)}, u32[]{:S(2)}) copy-start(bf16[192,2560]{1,0:T(8,128)(2,1)} %keys.1) | copy-start | bytes 2949124
  60.9 3.6 %copy-start.3 = (bf16[192,2560]{1,0:T(8,128)(2,1)S(1)}, bf16[192,2560]{1,0:T(8,128)(2,1)}, u32[]{:S(2)}) copy-start(bf16[192,2560]{1,0:T(8,128)(2,1)} %values.1) | copy-start | bytes 2949124
  62.9 93.9 %collective-permute-start.13 = (bf16[4,640,640]{2,1,0:T(8,128)(2,1)}, bf16[4,640,640]{2,1,0:T(8,128)(2,1)}, u32[]{:S(2)}, u32[]{:S(2)}) collective-permute-start(bf16[4,640,640]{2,1,0:T(8,128)(2,1)} %pad_maximum_fusion.refs_5_), channel_id=1, source_target_pairs={{0,64},{1,9},{2,66},{3,11},{4,68},{5,13},{6,70},{7,15},{8,72},{9,1... | collective-permute-start | bytes 9830408 | tf_op jit(solution)/shard_map/ppermute | solution.py:66
  63.1 95.3 %collective-permute-start.14 = (bf16[4,640,640]{2,1,0:T(8,128)(2,1)}, bf16[4,640,640]{2,1,0:T(8,128)(2,1)}, u32[]{:S(2)}, u32[]{:S(2)}) collective-permute-start(bf16[4,640,640]{2,1,0:T(8,128)(2,1)} %pad_maximum_fusion.refs_5_), channel_id=1, source_target_pairs={{0,192},{1,25},{2,194},{3,27},{4,196},{5,29},{6,198},{7,31},{8,200... | collective-permute-start | bytes 9830408 | tf_op jit(solution)/shard_map/ppermute | solution.py:66
  64.5 5.3 %copy-start.10 = (bf16[32,64,256]{2,1,0:T(8,128)(2,1)S(1)}, bf16[32,64,256]{2,1,0:T(8,128)(2,1)}, u32[]{:S(2)}) copy-start(bf16[32,64,256]{2,1,0:T(8,128)(2,1)} %copy-done.9) | copy-start | bytes 3145732
  68.8 1.0 copy-start
  69.8 1.0 copy-start.11
  86.2 9.7 %collective-permute-start.21 = (f32[16,120,128]{2,1,0:T(8,128)}, f32[16,120,128]{2,1,0:T(8,128)S(1)}, u32[]{:S(2)}, u32[]{:S(2)}) collective-permute-start(f32[16,120,128]{2,1,0:T(8,128)} %get-tuple-element.23), channel_id=1, source_target_pairs={{0,1},{1,0},{2,3},{3,2},{4,5},{5,4},{6,7},{7,6},{8,9},{9,8},{10,11... | collective-permute-start | bytes 2949128 | tf_op jit(solution)/shard_map/ppermute | solution.py:66
  97.3 27.0 %collective-permute-start.22 = (f32[8,120,128]{2,1,0:T(8,128)S(1)}, f32[8,120,128]{2,1,0:T(8,128)S(1)}, u32[]{:S(2)}, u32[]{:S(2)}) collective-permute-start(f32[8,120,128]{2,1,0:T(8,128)S(1)} %slice.59), channel_id=1, source_target_pairs={{0,4},{1,5},{2,6},{3,7},{4,0},{5,1},{6,2},{7,3},{8,12},{9,13},{10,... | collective-permute-start | bytes 1474568 | tf_op jit(solution)/shard_map/ppermute | solution.py:66
  124.4 9.7 %collective-permute-start.23 = (f32[4,120,128]{2,1,0:T(8,128)S(1)}, f32[4,120,128]{2,1,0:T(8,128)S(1)}, u32[]{:S(2)}, u32[]{:S(2)}) collective-permute-start(f32[4,120,128]{2,1,0:T(8,128)S(1)} %slice.61), channel_id=1, source_target_pairs={{0,2},{1,3},{2,0},{3,1},{4,6},{5,7},{6,4},{7,5},{8,10},{9,11},{10,... | collective-permute-start | bytes 737288 | tf_op jit(solution)/shard_map/ppermute | solution.py:66
  134.1 5.3 %collective-permute-start.24 = (f32[2,120,128]{2,1,0:T(8,128)S(1)}, f32[2,120,128]{2,1,0:T(8,128)S(1)}, u32[]{:S(2)}, u32[]{:S(2)}) collective-permute-start(f32[2,120,128]{2,1,0:T(8,128)S(1)} %slice.63), channel_id=1, source_target_pairs={{0,16},{1,17},{2,18},{3,19},{4,20},{5,21},{6,22},{7,23},{8,24},{9,... | collective-permute-start | bytes 368648 | tf_op jit(solution)/shard_map/ppermute | solution.py:66
  139.5 3.2 %collective-permute-start.25 = (f32[1,120,128]{2,1,0:T(8,128)S(1)}, f32[1,120,128]{2,1,0:T(8,128)S(1)}, u32[]{:S(2)}, u32[]{:S(2)}) collective-permute-start(f32[1,120,128]{2,1,0:T(8,128)S(1)} %slice.65), channel_id=1, source_target_pairs={{0,8},{1,9},{2,10},{3,11},{4,12},{5,13},{6,14},{7,15},{8,0},{9,1},... | collective-permute-start | bytes 184328 | tf_op jit(solution)/shard_map/ppermute | solution.py:66
  142.6 3.2 %collective-permute-start.26 = (f32[120,128]{1,0:T(8,128)S(1)}, f32[120,128]{1,0:T(8,128)S(1)}, u32[]{:S(2)}, u32[]{:S(2)}) collective-permute-start(f32[120,128]{1,0:T(8,128)S(1)} %fusion), channel_id=1, source_target_pairs={{0,64},{1,65},{2,66},{3,67},{4,68},{5,69},{6,70},{7,71},{8,72},{9,... | collective-permute-start | bytes 184328 | tf_op jit(solution)/shard_map/ppermute | solution.py:66
  145.8 5.0 %collective-permute-start.27 = (f32[120,128]{1,0:T(8,128)S(1)}, f32[120,128]{1,0:T(8,128)S(1)}, u32[]{:S(2)}, u32[]{:S(2)}) collective-permute-start(f32[120,128]{1,0:T(8,128)S(1)} %add.29), channel_id=1, source_target_pairs={{0,128},{1,129},{2,130},{3,131},{4,132},{5,133},{6,134},{7,135},{8... | collective-permute-start | bytes 184328 | tf_op jit(solution)/shard_map/ppermute | solution.py:66
  150.8 9.7 %collective-permute-start.28 = (f32[120,128]{1,0:T(8,128)S(1)}, f32[120,128]{1,0:T(8,128)S(1)}, u32[]{:S(2)}, u32[]{:S(2)}) collective-permute-start(f32[120,128]{1,0:T(8,128)S(1)} %add.30), channel_id=1, source_target_pairs={{0,32},{1,33},{2,34},{3,35},{4,36},{5,37},{6,38},{7,39},{8,40},{9,... | collective-permute-start | bytes 184328 | tf_op jit(solution)/shard_map/ppermute | solution.py:66
  150.9 35.1 %collective-permute-start.12 = (bf16[4,640,640]{2,1,0:T(8,128)(2,1)}, bf16[4,640,640]{2,1,0:T(8,128)(2,1)}, u32[]{:S(2)}, u32[]{:S(2)}) collective-permute-start(bf16[4,640,640]{2,1,0:T(8,128)(2,1)} %pad_maximum_fusion.refs_5_), channel_id=1, source_target_pairs={{0,1},{1,0},{2,3},{3,2},{4,5},{5,4},{6,7},{7,6},{8,9},{9,8},{10,11... | collective-permute-start | bytes 9830408 | tf_op jit(solution)/shard_map/ppermute | solution.py:66
  156.7 44.4 %collective-permute-start.15 = (bf16[4,640,640]{2,1,0:T(8,128)(2,1)}, bf16[4,640,640]{2,1,0:T(8,128)(2,1)S(1)}, u32[]{:S(2)}, u32[]{:S(2)}) collective-permute-start(bf16[4,640,640]{2,1,0:T(8,128)(2,1)} %collective-permute-done.13.refs_5_), channel_id=1, source_target_pairs={{0,1},{1,0},{2,3},{3,2},{4,5},{5,4},{6,7},{7,6},{8,9},{9,8},{10,11... | collective-permute-start | bytes 9830408 | tf_op jit(solution)/shard_map/ppermute | solution.py:66
  158.4 42.7 %collective-permute-start.16 = (bf16[4,640,640]{2,1,0:T(8,128)(2,1)}, bf16[4,640,640]{2,1,0:T(8,128)(2,1)}, u32[]{:S(2)}, u32[]{:S(2)}) collective-permute-start(bf16[4,640,640]{2,1,0:T(8,128)(2,1)} %collective-permute-done.14.refs_6_), channel_id=1, source_target_pairs={{0,1},{1,0},{2,3},{3,2},{4,5},{5,4},{6,7},{7,6},{8,9},{9,8},{10,11... | collective-permute-start | bytes 9830408 | tf_op jit(solution)/shard_map/ppermute | solution.py:66
  158.9 20.4 %collective-permute-start.17 = (bf16[2,640,640]{2,1,0:T(8,128)(2,1)S(1)}, bf16[2,640,640]{2,1,0:T(8,128)(2,1)}, u32[]{:S(2)}, u32[]{:S(2)}) collective-permute-start(bf16[2,640,640]{2,1,0:T(8,128)(2,1)S(1)} %slice.56), channel_id=1, source_target_pairs={{0,64},{1,9},{2,66},{3,11},{4,68},{5,13},{6,70},{7,15},{8,72},{9,1... | collective-permute-start | bytes 4915208 | tf_op jit(solution)/shard_map/ppermute | solution.py:66
  160.5 21.7 %collective-permute-start.18 = (bf16[2,640,640]{2,1,0:T(8,128)(2,1)S(1)}, bf16[2,640,640]{2,1,0:T(8,128)(2,1)}, u32[]{:S(2)}, u32[]{:S(2)}) collective-permute-start(bf16[2,640,640]{2,1,0:T(8,128)(2,1)S(1)} %slice.57), channel_id=1, source_target_pairs={{0,192},{1,25},{2,194},{3,27},{4,196},{5,29},{6,198},{7,31},{8,200... | collective-permute-start | bytes 4915208 | tf_op jit(solution)/shard_map/ppermute | solution.py:66
  179.3 47.0 %collective-permute-start.19 = (bf16[2,640,640]{2,1,0:T(8,128)(2,1)}, bf16[2,640,640]{2,1,0:T(8,128)(2,1)}, u32[]{:S(2)}, u32[]{:S(2)}) collective-permute-start(bf16[2,640,640]{2,1,0:T(8,128)(2,1)} %collective-permute-done.17.refs_5_), channel_id=1, source_target_pairs={{0,1},{1,0},{2,3},{3,2},{4,5},{5,4},{6,7},{7,6},{8,9},{9,8},{10,11... | collective-permute-start | bytes 4915208 | tf_op jit(solution)/shard_map/ppermute | solution.py:66
  182.2 44.2 %collective-permute-start.20 = (bf16[2,640,640]{2,1,0:T(8,128)(2,1)}, bf16[2,640,640]{2,1,0:T(8,128)(2,1)}, u32[]{:S(2)}, u32[]{:S(2)}) collective-permute-start(bf16[2,640,640]{2,1,0:T(8,128)(2,1)} %collective-permute-done.18.refs_6_), channel_id=1, source_target_pairs={{0,1},{1,0},{2,3},{3,2},{4,5},{5,4},{6,7},{7,6},{8,9},{9,8},{10,11... | collective-permute-start | bytes 4915208 | tf_op jit(solution)/shard_map/ppermute | solution.py:66
  201.1 1.7 copy-start.8
